TPU v7x, 32 devices: a whole 2x2x4 slice. The times are simulated.
32 devices in a mesh: batch: 4 (over x, core), centers: 8 (over z, y).
Axes of the slice: x: 2, y: 2, z: 4, core: 2. Of those that a mesh axis runs over, the one named last changes fastest.
Arguments:
- pool_features: float32 [32768, 128], P(('batch', 'centers')), may hold values from -14 to 14
- pool_targets: float32 [32768, 64], P(('batch', 'centers')), may hold values from -6 to 6
- batch_index: int32 [2048], P(('batch', 'centers')), may hold values from 0 to 1023
- centers: float32 [4096, 128], P('centers'), may hold values from -14 to 14
- weights: float32 [4096, 64], P('centers'), as said below
- eig_vectors: float32 [4096, 1024], P(('batch', 'centers')), may hold values from -0.09375 to 0.09375
- eig_scale: float32 [1024], replicated, may hold values from 0.5 to 4
- nys_owner: int32 [4096, 1], P(('batch', 'centers')), may hold values from 0 to 7; in each aligned block of 128 rows (0 to 127, 128 to 255, ...) at most 32 rows name the same one
- nys_offset: int32 [4096], P(('batch', 'centers')), may hold values from 0 to 511
Outputs:
- residual_out: float32 [2048, 64], P(('batch', 'centers'))
- update: float32 [4096, 64], P('centers')
Inputs may be any that keep to these rules, and one draw needn't show every extreme that they name: `nys_owner`: among the 128 rows of one device no owner is named more than 32 times; on some devices one owner is named exactly 32 times. `weights`: every column sums to zero.
All inputs are finite; a program needn't handle non-finite values.
Results may differ from a plain program's by a relative error of at most 0.0003.
Values sent between devices are 32-bit elements; how exact they have to be, the bound alone decides.
A program may use at most 64 MiB of HBM per device.

v0:
```python
import math
import jax
import jax.numpy as jnp
from jax import lax
from jax.sharding import PartitionSpec as P

DEPTH = 3
epsilon = 1e-06
highest = lax.Precision.HIGHEST


def kernel_rows(row_block, center_block, center_norm):
    inner_prod = (
        lax.dot_general(
            row_block,
            center_block,
            (((1,), (1,)), ((), ())),
            precision=highest,
            preferred_element_type=jnp.float32,
        )
        / row_block.shape[1]
    )
    row_norm = jnp.mean(row_block * row_block, axis=1) + epsilon
    norm_scale = jnp.sqrt(row_norm[:, None] * center_norm[None, :])
    sigma_now = inner_prod
    tangent = inner_prod
    for depth_step in range(DEPTH):
        cosine = sigma_now / norm_scale
        arc_angle = jnp.arccos(cosine)
        remain = (math.pi - arc_angle) / math.pi
        sigma_now = (
            norm_scale
            * (jnp.sqrt(1.0 - cosine * cosine) + (math.pi - arc_angle) * cosine)
            / math.pi
        )
        tangent = sigma_now + tangent * remain
    return tangent


def per_device(
    pool_features,
    pool_targets,
    batch_index,
    centers,
    weights,
    eig_vectors,
    eig_scale,
    nys_owner,
    nys_offset,
):
    local_rows = pool_features[batch_index]
    local_targets = pool_targets[batch_index]
    row_count = local_rows.shape[0]
    group_size = lax.axis_size("centers")
    rows_total = row_count * group_size * lax.axis_size("batch")
    center_count = centers.shape[0]
    outputs = weights.shape[1]
    center_norm = jnp.mean(centers * centers, axis=1) + epsilon
    kernel = kernel_rows(
        lax.all_gather(local_rows, "centers", axis=0, tiled=True), centers, center_norm
    )
    partial_pred = jnp.dot(kernel, weights, precision=highest, preferred_element_type=jnp.float32)
    all_targets = lax.all_gather(local_targets, "centers", axis=0, tiled=True)
    prediction = lax.psum(partial_pred, "centers")
    residual = prediction - all_targets
    own_residual = lax.dynamic_slice_in_dim(
        residual, lax.axis_index("centers") * row_count, row_count, 0
    )
    grads_part = lax.dot_general(
        kernel,
        residual,
        (((0,), (0,)), ((), ())),
        precision=highest,
        preferred_element_type=jnp.float32,
    ) / math.sqrt(rows_total)
    grads = lax.psum(grads_part, "batch")
    owner = nys_owner[:, 0]
    slots = max(2, 2 * owner.shape[0] // group_size)
    owner_hot = (owner[:, None] == jnp.arange(group_size, dtype=jnp.int32)[None, :]).astype(
        jnp.int32
    )
    slot_rank = jnp.sum((jnp.cumsum(owner_hot, axis=0) - owner_hot) * owner_hot, axis=1)
    requests = jnp.zeros((group_size, slots), jnp.int32).at[owner, slot_rank].set(nys_offset)
    received = lax.all_to_all(requests, "centers", split_axis=0, concat_axis=0, tiled=True)
    found = grads[received]
    returned = lax.all_to_all(found, "centers", split_axis=0, concat_axis=0, tiled=True)
    picked_grads = returned[owner, slot_rank]
    coeff_part = lax.dot_general(
        eig_vectors,
        picked_grads,
        (((0,), (0,)), ((), ())),
        precision=highest,
        preferred_element_type=jnp.float32,
    )
    coeff = lax.psum(coeff_part, ("batch", "centers"))
    corr_rows = jnp.dot(
        eig_vectors,
        eig_scale[:, None] * coeff,
        precision=highest,
        preferred_element_type=jnp.float32,
    )
    outgoing = (
        jnp.zeros((group_size, slots, outputs), jnp.float32).at[owner, slot_rank].set(corr_rows)
    )
    incoming = lax.all_to_all(outgoing, "centers", split_axis=0, concat_axis=0, tiled=True)
    corr_part = jnp.zeros((center_count, outputs), jnp.float32).at[received].add(incoming)
    correction = lax.psum(corr_part, "batch")
    return (own_residual, correction - grads)


def solution(mesh):
    placed = (
        P(("batch", "centers"), None),
        P(("batch", "centers"), None),
        P(("batch", "centers")),
        P("centers", None),
        P("centers", None),
        P(("batch", "centers"), None),
        P(),
        P(("batch", "centers"), None),
        P(("batch", "centers")),
    )
    return jax.shard_map(
        per_device,
        mesh=mesh,
        in_specs=placed,
        out_specs=(P(("batch", "centers"), None), P("centers", None)),
        check_vma=False,
    )
```

profile of v0, /device:TPU:0, one launch (start us, length us, event | category | flops | bytes accessed | tf_op | source)
XLA Modules:
  0.0 387.0 jit_solution(5106888059048131326)
XLA Ops:
  9.0 19.9 %scatter_fusion = s32[8,32]{1,0:T(8,128)} fusion(s32[8,32]{1,0:T(8,128)} %broadcast.104, s32[128]{0:T(128)S(1)} %get-tuple-element.8, s32[128]{0:T(128)S(1)} %copy-done.8), kind=kCustom, calls=%fused_computation.4 | custom fusion | bytes 2560 | tf_op jit(solution)/shard_map/scatter | solution.py:83
  28.9 7.4 %all-to-all-start = ((s32[8,1,32]{2,1,0:T(1,128)}), s32[8,1,32]{2,1,0:T(1,128)S(1)}, u32[]{:S(2)}, u32[]{:S(2)}) async-start(s32[8,1,32]{2,1,0:T(1,128)} %bitcast.4), calls=%async_computation | async-start | bytes 8192 | tf_op jit(solution)/shard_map/all_to_all | solution.py:84
  37.2 31.2 %all-gather = f32[512,128]{1,0:T(8,128)S(1)} all-gather(f32[64,128]{1,0:T(8,128)S(1)} %gather_fusion), channel_id=2, replica_groups=mesh['batch'=4,'centers'=8] {'centers'}, dimensions={0}, use_global_device_ids=true | all-gather | bytes 294912 | tf_op jit(solution)/shard_map/all_gather | solution.py:60
  68.6 8.9 %multiply_add_fusion = f32[512,512]{1,0:T(8,128)S(1)} fusion(f32[512,128]{1,0:T(8,128)S(1)} %all-gather, f32[512,128]{1,0:T(8,128)S(1)} %copy-done.3, f32[512]{0:T(512)S(1)} %multiply_add_fusion.1, f32[512]{0:T(512)S(1)} %multiply_add_fusion.2), kind=kOutput, calls=%fused_computation.11 | convolution fusion | flops 414187520 | bytes 1576960 | tf_op jit(solution)/shard_map/dot_general | solution.py:14
  77.5 1.8 fusion.8
  80.2 30.8 %all-gather.1 = f32[512,64]{1,0:T(8,128)S(1)} all-gather(f32[64,64]{1,0:T(8,128)S(1)} %gather_fusion.1), channel_id=3, replica_groups=mesh['batch'=4,'centers'=8] {'centers'}, dimensions={0}, use_global_device_ids=true | all-gather | bytes 147456 | tf_op jit(solution)/shard_map/all_gather | solution.py:63
  111.3 39.5 %all-reduce.5.cloned.1.call-done = f32[512,64]{0,1:T(8,128)} async-done(((f32[512,64]{0,1:T(8,128)}), f32[512,64]{0,1:T(8,128)}) %all-reduce.5.cloned.1.call-update) | async-done | bytes 131088 | tf_op jit(solution)/shard_map/psum | solution.py:64
  150.8 0.9 sub.36
  151.7 1.5 convolution_multiply_fusion.1
  153.3 31.3 %all-reduce.7.cloned.1.call-done = f32[512,64]{0,1:T(8,128)} async-done(((f32[512,64]{0,1:T(8,128)}), f32[512,64]{0,1:T(8,128)}) %all-reduce.7.cloned.1.call-update) | async-done | bytes 131088 | tf_op jit(solution)/shard_map/psum | solution.py:76
  184.6 1.0 copy.26
  186.5 12.2 %all_to_all.22 = f32[8,1,2048]{2,1,0:T(1,128)S(1)} all-to-all(f32[8,1,2048]{2,1,0:T(1,128)S(1)} %reshape.114), channel_id=1, replica_groups=mesh['batch'=4,'centers'=8] {'centers'}, dimensions={0} | all-to-all | bytes 131072 | tf_op jit(solution)/shard_map/all_to_all | solution.py:86
  199.2 0.8 reduce
  200.1 1.2 gather_fusion.3
  201.3 1.1 convolution_bitcast_fusion
  202.5 123.4 %all-reduce.9.cloned.1.call-done = f32[1024,64]{0,1:T(8,128)} async-done(((f32[1024,64]{0,1:T(8,128)}), f32[1024,64]{0,1:T(8,128)}) %all-reduce.9.cloned.1.call-update) | async-done | bytes 262160 | tf_op jit(solution)/shard_map/psum | solution.py:95
  325.9 1.6 convolution_bitcast_fusion.1
  327.7 6.9 %scatter_fusion.1 = f32[8,32,64]{2,1,0:T(8,128)S(1)} fusion(f32[8,32,64]{2,1,0:T(8,128)S(1)} %broadcast_in_dim.8, s32[128]{0:T(128)S(1)} %get-tuple-element.8, f32[128,64]{1,0:T(8,128)S(1)} %copy.27), kind=kCustom, calls=%fused_computation.5 | custom fusion | bytes 99328 | tf_op jit(solution)/shard_map/scatter | solution.py:103
  335.3 4.5 %all-to-all-start.2 = ((f32[8,1,2048]{2,1,0:T(1,128)}), f32[8,1,2048]{2,1,0:T(1,128)S(1)}, u32[]{:S(2)}, u32[]{:S(2)}) async-start(f32[8,1,2048]{2,1,0:T(1,128)} %reshape.116), calls=%async_computation.2 | async-start | bytes 131072 | tf_op jit(solution)/shard_map/all_to_all | solution.py:105
  339.9 6.9 %all-to-all-done.2 = f32[8,1,2048]{2,1,0:T(1,128)S(1)} async-done(((f32[8,1,2048]{2,1,0:T(1,128)}), f32[8,1,2048]{2,1,0:T(1,128)S(1)}, u32[]{:S(2)}, u32[]{:S(2)}) %all-to-all-start.2) | async-done | bytes 65568 | tf_op jit(solution)/shard_map/all_to_all | solution.py:105
  346.7 0.8 reduce.1
  347.6 1.7 scatter_custom_fusion.2
  351.0 27.9 %all-reduce.11.cloned.1.call-done = f32[512,64]{0,1:T(8,128)} async-done(((f32[512,64]{0,1:T(8,128)}), f32[512,64]{0,1:T(8,128)}) %all-reduce.11.cloned.1.call-update) | async-done | bytes 131088 | tf_op jit(solution)/shard_map/psum | solution.py:107
  378.9 1.6 sub.38
  (58 shorter events, 7.9 us)
Async XLA Ops:
  7.2 194.2 %copy-start = (f32[128,1024]{1,0:T(8,128)S(1)}, f32[128,1024]{1,0:T(8,128)}, u32[]{:S(2)}) copy-start(f32[128,1024]{1,0:T(8,128)} %param.14) | copy-start | bytes 1572868
  7.2 0.7 copy-start.6
  8.3 0.7 copy-start.8
  9.0 27.4 %copy-start.3 = (f32[512,128]{1,0:T(8,128)S(1)}, f32[512,128]{1,0:T(8,128)}, u32[]{:S(2)}) copy-start(f32[512,128]{1,0:T(8,128)} %param.12) | copy-start | bytes 786436
  9.0 27.6 %copy-start.5 = (f32[1024,128]{1,0:T(8,128)S(1)}, f32[1024,128]{1,0:T(8,128)}, u32[]{:S(2)}) copy-start(f32[1024,128]{1,0:T(8,128)} %param.9) | copy-start | bytes 1572868
  28.9 7.5 %copy-start.9 = (s32[64]{0:T(128)S(1)}, s32[64]{0:T(128)}, u32[]{:S(2)}) copy-start(s32[64]{0:T(128)} %param.11) | copy-start | bytes 772
  28.9 82.3 %all-to-all-start = ((s32[8,1,32]{2,1,0:T(1,128)}), s32[8,1,32]{2,1,0:T(1,128)S(1)}, u32[]{:S(2)}, u32[]{:S(2)}) async-start(s32[8,1,32]{2,1,0:T(1,128)} %bitcast.4), calls=%async_computation | async-start | bytes 8192 | tf_op jit(solution)/shard_map/all_to_all | solution.py:84
  36.3 114.5 %all-reduce.5.cloned.1.call-start = ((), (), s32[]{:S(2)}) async-start(), calls=%async_computation.3 | async-start | bytes 262144 | tf_op jit(solution)/shard_map/psum | solution.py:64
  68.6 8.9 %copy-start.4 = (f32[512,64]{0,1:T(8,128)S(1)}, f32[512,64]{0,1:T(8,128)}, u32[]{:S(2)}) copy-start(f32[512,64]{0,1:T(8,128)} %param.13) | copy-start | bytes 393220
  77.5 1.9 copy-start.2
  79.4 105.2 %all-reduce.7.cloned.1.call-start = ((), (), s32[]{:S(2)}) async-start(), calls=%async_computation.4 | async-start | bytes 262144 | tf_op jit(solution)/shard_map/psum | solution.py:76
  153.2 172.7 %all-reduce.9.cloned.1.call-start = ((), (), s32[]{:S(2)}) async-start(), calls=%async_computation.5 | async-start | bytes 524288 | tf_op jit(solution)/shard_map/psum | solution.py:95
  202.5 123.4 %copy-start.7 = (f32[1024]{0:T(1024)S(1)}, f32[1024]{0:T(1024)}, u32[]{:S(2)}) copy-start(f32[1024]{0:T(1024)} %param.15) | copy-start | bytes 12292
  335.3 11.4 %all-to-all-start.2 = ((f32[8,1,2048]{2,1,0:T(1,128)}), f32[8,1,2048]{2,1,0:T(1,128)S(1)}, u32[]{:S(2)}, u32[]{:S(2)}) async-start(f32[8,1,2048]{2,1,0:T(1,128)} %reshape.116), calls=%async_computation.2 | async-start | bytes 131072 | tf_op jit(solution)/shard_map/all_to_all | solution.py:105
  339.8 39.0 %all-reduce.11.cloned.1.call-start = ((), (), s32[]{:S(2)}) async-start(), calls=%async_computation.6 | async-start | bytes 262144 | tf_op jit(solution)/shard_map/psum | solution.py:107
  350.1 28.7 %copy-start.1 = (f32[512,64]{0,1:T(8,128)S(1)}, f32[512,64]{0,1:T(8,128)}, u32[]{:S(2)}) copy-start(f32[512,64]{0,1:T(8,128)} %all-reduce.7.cloned.1.call-done) | copy-start | bytes 393220
Sparse Core Ops, SparseCore 0:
  79.5 71.2 all-reduce.4
  153.7 30.8 all-reduce.6
  202.6 123.2 all-reduce.8
  350.3 28.5 all-reduce.10
where the time goes:
time: 388 us; the launch traced here: 387 us
  waiting for transfers between devices  229 us (59%)
  blocking collectives  74.3 us (19%)
  local copies, waits for them, and re-layouts  36 us (9%)
  matrix products  14.9 us (4%)
  between operations  14 us (4%)
  starting transfers between devices  12.1 us (3%)
  other arithmetic  6.6 us (2%)
    psum x1, waiting for transfers between devices, per_device(): coeff = lax.psum(coeff_part, ('batch', 'centers'))  123 us
    psum x1, waiting for transfers between devices, per_device(): prediction = lax.psum(partial_pred, 'centers')  39.5 us
    psum x1, waiting for transfers between devices, per_device(): grads = lax.psum(grads_part, 'batch')  31.3 us
    all_gather x1, blocking collectives, per_device(): lax.all_gather(local_rows, 'centers', axis=0, tiled=True)  31.2 us
    all_gather x1, blocking collectives, per_device(): all_targets = lax.all_gather(local_targets, 'centers', axis=0, tiled=True)  30.8 us
    psum x1, waiting for transfers between devices, per_device(): correction = lax.psum(corr_part, 'batch')  27.9 us
    scatter x1, local copies, waits for them, and re-layouts, per_device(): jnp.zeros((group_size, slots), jnp.int32).at[owner, slot_rank]  19.9 us
    all_to_all x1, blocking collectives, per_device(): lax.all_to_all(found, 'centers', split_axis=0, concat_axis=0, tiled=True)  12.2 us
  transfers between devices with their start and end apart: 6, of which 5 were waited for; matrix products, arithmetic and copies ran while one was open for 3% of the time, Pallas kernels for 0%

commit v1 on v0

--- a/solution.py
+++ b/solution.py
@@ -92,7 +92,7 @@
         precision=highest,
         preferred_element_type=jnp.float32,
     )
-    coeff = lax.psum(coeff_part, ("batch", "centers"))
+    coeff = lax.psum(lax.psum(coeff_part, "batch"), "centers")
     corr_rows = jnp.dot(
         eig_vectors,
         eig_scale[:, None] * coeff,

time: 388 us -> 368 us (0.948)
  waiting for transfers between devices: 229 us -> 210 us
    psum x1 -> x2, waiting for transfers between devices: 123 us -> 103 us  [per_device(): coeff = lax.psum(lax.psum(coeff_part, 'batch'), 'centers')]
  transfers between devices with their start and end apart: 6 -> 7, of which waited for: 5 -> 6; matrix products, arithmetic and copies ran while one was open for 3% -> 4% of each run, Pallas kernels for 0% -> 0%
where the time goes in v1:
time: 368 us; the launch traced here: 367 us
  waiting for transfers between devices  210 us (57%)
  blocking collectives  74.3 us (20%)
  local copies, waits for them, and re-layouts  36 us (10%)
  matrix products  14.9 us (4%)
  between operations  14 us (4%)
  starting transfers between devices  11.4 us (3%)
  other arithmetic  6.6 us (2%)
    psum x2, waiting for transfers between devices, per_device(): coeff = lax.psum(lax.psum(coeff_part, 'batch'), 'centers')  103 us
    psum x1, waiting for transfers between devices, per_device(): prediction = lax.psum(partial_pred, 'centers')  39.5 us
    psum x1, waiting for transfers between devices, per_device(): grads = lax.psum(grads_part, 'batch')  31.3 us
    all_gather x1, blocking collectives, per_device(): lax.all_gather(local_rows, 'centers', axis=0, tiled=True)  31.2 us
    all_gather x1, blocking collectives, per_device(): all_targets = lax.all_gather(local_targets, 'centers', axis=0, tiled=True)  30.8 us
    psum x1, waiting for transfers between devices, per_device(): correction = lax.psum(corr_part, 'batch')  28.8 us
    scatter x1, local copies, waits for them, and re-layouts, per_device(): jnp.zeros((group_size, slots), jnp.int32).at[owner, slot_rank]  19.9 us
    all_to_all x1, blocking collectives, per_device(): lax.all_to_all(found, 'centers', split_axis=0, concat_axis=0, tiled=True)  12.2 us
  transfers between devices with their start and end apart: 7, of which 6 were waited for; matrix products, arithmetic and copies ran while one was open for 4% of the time, Pallas kernels for 0%

profile of v1, /device:TPU:0, one launch (start us, length us, event | category | flops | bytes accessed | tf_op | source)
XLA Modules:
  0.0 367.0 jit_solution(14997561860119243724)
XLA Ops:
  9.0 19.9 %scatter_fusion = s32[8,32]{1,0:T(8,128)} fusion(s32[8,32]{1,0:T(8,128)} %broadcast.104, s32[128]{0:T(128)S(1)} %get-tuple-element.8, s32[128]{0:T(128)S(1)} %copy-done.8), kind=kCustom, calls=%fused_computation.4 | custom fusion | bytes 2560 | tf_op jit(solution)/shard_map/scatter | solution.py:83
  28.9 7.4 %all-to-all-start = ((s32[8,1,32]{2,1,0:T(1,128)}), s32[8,1,32]{2,1,0:T(1,128)S(1)}, u32[]{:S(2)}, u32[]{:S(2)}) async-start(s32[8,1,32]{2,1,0:T(1,128)} %bitcast.4), calls=%async_computation | async-start | bytes 8192 | tf_op jit(solution)/shard_map/all_to_all | solution.py:84
  37.2 31.2 %all-gather = f32[512,128]{1,0:T(8,128)S(1)} all-gather(f32[64,128]{1,0:T(8,128)S(1)} %gather_fusion), channel_id=2, replica_groups=mesh['batch'=4,'centers'=8] {'centers'}, dimensions={0}, use_global_device_ids=true | all-gather | bytes 294912 | tf_op jit(solution)/shard_map/all_gather | solution.py:60
  68.6 8.9 %multiply_add_fusion = f32[512,512]{1,0:T(8,128)S(1)} fusion(f32[512,128]{1,0:T(8,128)S(1)} %all-gather, f32[512,128]{1,0:T(8,128)S(1)} %copy-done.3, f32[512]{0:T(512)S(1)} %multiply_add_fusion.1, f32[512]{0:T(512)S(1)} %multiply_add_fusion.2), kind=kOutput, calls=%fused_computation.11 | convolution fusion | flops 414187520 | bytes 1576960 | tf_op jit(solution)/shard_map/dot_general | solution.py:14
  77.5 1.8 fusion.8
  80.2 30.8 %all-gather.1 = f32[512,64]{1,0:T(8,128)S(1)} all-gather(f32[64,64]{1,0:T(8,128)S(1)} %gather_fusion.1), channel_id=3, replica_groups=mesh['batch'=4,'centers'=8] {'centers'}, dimensions={0}, use_global_device_ids=true | all-gather | bytes 147456 | tf_op jit(solution)/shard_map/all_gather | solution.py:63
  111.3 39.5 %all-reduce.6.cloned.1.call-done = f32[512,64]{0,1:T(8,128)} async-done(((f32[512,64]{0,1:T(8,128)}), f32[512,64]{0,1:T(8,128)}) %all-reduce.6.cloned.1.call-update) | async-done | bytes 131088 | tf_op jit(solution)/shard_map/psum | solution.py:64
  150.8 0.9 sub.36
  151.7 1.5 convolution_multiply_fusion.1
  153.3 31.3 %all-reduce.8.cloned.1.call-done = f32[512,64]{0,1:T(8,128)} async-done(((f32[512,64]{0,1:T(8,128)}), f32[512,64]{0,1:T(8,128)}) %all-reduce.8.cloned.1.call-update) | async-done | bytes 131088 | tf_op jit(solution)/shard_map/psum | solution.py:76
  184.6 1.0 copy.26
  186.5 12.2 %all_to_all.22 = f32[8,1,2048]{2,1,0:T(1,128)S(1)} all-to-all(f32[8,1,2048]{2,1,0:T(1,128)S(1)} %reshape.114), channel_id=1, replica_groups=mesh['batch'=4,'centers'=8] {'centers'}, dimensions={0} | all-to-all | bytes 131072 | tf_op jit(solution)/shard_map/all_to_all | solution.py:86
  199.2 0.8 reduce
  200.1 1.2 gather_fusion.3
  201.3 1.1 convolution_bitcast_fusion
  202.5 29.0 %all-reduce.10.cloned.1.call-done = f32[1024,64]{0,1:T(8,128)} async-done(((f32[1024,64]{0,1:T(8,128)}), f32[1024,64]{0,1:T(8,128)}) %all-reduce.10.cloned.1.call-update) | async-done | bytes 262160 | tf_op jit(solution)/shard_map/psum | solution.py:95
  231.5 74.2 %all-reduce.12.cloned.1.call-done = f32[1024,64]{0,1:T(8,128)} async-done(((f32[1024,64]{0,1:T(8,128)}), f32[1024,64]{0,1:T(8,128)}) %all-reduce.12.cloned.1.call-update) | async-done | bytes 262160 | tf_op jit(solution)/shard_map/psum | solution.py:95
  305.8 1.6 convolution_bitcast_fusion.1
  307.5 6.9 %scatter_fusion.1 = f32[8,32,64]{2,1,0:T(8,128)S(1)} fusion(f32[8,32,64]{2,1,0:T(8,128)S(1)} %broadcast_in_dim.8, s32[128]{0:T(128)S(1)} %get-tuple-element.8, f32[128,64]{1,0:T(8,128)S(1)} %copy.27), kind=kCustom, calls=%fused_computation.5 | custom fusion | bytes 99328 | tf_op jit(solution)/shard_map/scatter | solution.py:103
  315.2 3.8 %all-to-all-start.2 = ((f32[8,1,2048]{2,1,0:T(1,128)}), f32[8,1,2048]{2,1,0:T(1,128)S(1)}, u32[]{:S(2)}, u32[]{:S(2)}) async-start(f32[8,1,2048]{2,1,0:T(1,128)} %reshape.116), calls=%async_computation.2 | async-start | bytes 131072 | tf_op jit(solution)/shard_map/all_to_all | solution.py:105
  319.0 6.9 %all-to-all-done.2 = f32[8,1,2048]{2,1,0:T(1,128)S(1)} async-done(((f32[8,1,2048]{2,1,0:T(1,128)}), f32[8,1,2048]{2,1,0:T(1,128)S(1)}, u32[]{:S(2)}, u32[]{:S(2)}) %all-to-all-start.2) | async-done | bytes 65568 | tf_op jit(solution)/shard_map/all_to_all | solution.py:105
  326.8 1.7 scatter_custom_fusion.2
  330.1 28.8 %all-reduce.14.cloned.1.call-done = f32[512,64]{0,1:T(8,128)} async-done(((f32[512,64]{0,1:T(8,128)}), f32[512,64]{0,1:T(8,128)}) %all-reduce.14.cloned.1.call-update) | async-done | bytes 131088 | tf_op jit(solution)/shard_map/psum | solution.py:107
  358.9 1.6 sub.38
  (61 shorter events, 8.8 us)
Async XLA Ops:
  7.2 194.2 %copy-start = (f32[128,1024]{1,0:T(8,128)S(1)}, f32[128,1024]{1,0:T(8,128)}, u32[]{:S(2)}) copy-start(f32[128,1024]{1,0:T(8,128)} %param.14) | copy-start | bytes 1572868
  7.2 0.7 copy-start.6
  8.3 0.7 copy-start.8
  9.0 27.4 %copy-start.3 = (f32[512,128]{1,0:T(8,128)S(1)}, f32[512,128]{1,0:T(8,128)}, u32[]{:S(2)}) copy-start(f32[512,128]{1,0:T(8,128)} %param.12) | copy-start | bytes 786436
  9.0 27.6 %copy-start.5 = (f32[1024,128]{1,0:T(8,128)S(1)}, f32[1024,128]{1,0:T(8,128)}, u32[]{:S(2)}) copy-start(f32[1024,128]{1,0:T(8,128)} %param.9) | copy-start | bytes 1572868
  28.9 7.5 %copy-start.9 = (s32[64]{0:T(128)S(1)}, s32[64]{0:T(128)}, u32[]{:S(2)}) copy-start(s32[64]{0:T(128)} %param.11) | copy-start | bytes 772
  28.9 82.3 %all-to-all-start = ((s32[8,1,32]{2,1,0:T(1,128)}), s32[8,1,32]{2,1,0:T(1,128)S(1)}, u32[]{:S(2)}, u32[]{:S(2)}) async-start(s32[8,1,32]{2,1,0:T(1,128)} %bitcast.4), calls=%async_computation | async-start | bytes 8192 | tf_op jit(solution)/shard_map/all_to_all | solution.py:84
  36.3 114.5 %all-reduce.6.cloned.1.call-start = ((), (), s32[]{:S(2)}) async-start(), calls=%async_computation.3 | async-start | bytes 262144 | tf_op jit(solution)/shard_map/psum | solution.py:64
  68.6 8.9 %copy-start.4 = (f32[512,64]{0,1:T(8,128)S(1)}, f32[512,64]{0,1:T(8,128)}, u32[]{:S(2)}) copy-start(f32[512,64]{0,1:T(8,128)} %param.13) | copy-start | bytes 393220
  77.5 1.9 copy-start.2
  79.4 105.2 %all-reduce.8.cloned.1.call-start = ((), (), s32[]{:S(2)}) async-start(), calls=%async_computation.4 | async-start | bytes 262144 | tf_op jit(solution)/shard_map/psum | solution.py:76
  153.2 78.3 %all-reduce.10.cloned.1.call-start = ((), (), s32[]{:S(2)}) async-start(), calls=%async_computation.5 | async-start | bytes 524288 | tf_op jit(solution)/shard_map/psum | solution.py:95
  202.5 103.3 %all-reduce.12.cloned.1.call-start = ((), (), s32[]{:S(2)}) async-start(), calls=%async_computation.6 | async-start | bytes 524288 | tf_op jit(solution)/shard_map/psum | solution.py:95
  231.5 74.3 %copy-start.7 = (f32[1024]{0:T(1024)S(1)}, f32[1024]{0:T(1024)}, u32[]{:S(2)}) copy-start(f32[1024]{0:T(1024)} %param.15) | copy-start | bytes 12292
  315.2 10.7 %all-to-all-start.2 = ((f32[8,1,2048]{2,1,0:T(1,128)}), f32[8,1,2048]{2,1,0:T(1,128)S(1)}, u32[]{:S(2)}, u32[]{:S(2)}) async-start(f32[8,1,2048]{2,1,0:T(1,128)} %reshape.116), calls=%async_computation.2 | async-start | bytes 131072 | tf_op jit(solution)/shard_map/all_to_all | solution.py:105
  319.0 39.9 %all-reduce.14.cloned.1.call-start = ((), (), s32[]{:S(2)}) async-start(), calls=%async_computation.7 | async-start | bytes 262144 | tf_op jit(solution)/shard_map/psum | solution.py:107
  329.3 29.6 %copy-start.1 = (f32[512,64]{0,1:T(8,128)S(1)}, f32[512,64]{0,1:T(8,128)}, u32[]{:S(2)}) copy-start(f32[512,64]{0,1:T(8,128)} %all-reduce.8.cloned.1.call-done) | copy-start | bytes 393220
Sparse Core Ops, SparseCore 0:
  79.5 71.2 all-reduce.5
  153.7 30.8 all-reduce.7
  202.6 28.8 all-reduce.9
  234.7 71.0 all-reduce.11
  329.4 29.3 all-reduce.13
